TPU v7x, 32 devices: a whole 2x2x4 slice. The times are simulated.
32 devices in a mesh: fn: 8 (over z, x), sub: 4 (over y, core).
Axes of the slice: x: 2, y: 2, z: 4, core: 2. Of those that a mesh axis runs over, the one named last changes fastest.
Arguments:
- coeffs: float32 [1024, 4, 16, 128], P('fn', None, 'sub'), may hold values from -6 to 6
- offsets: int32 [1024], replicated, may hold values from 0 to 127, as said below
- potential: float32 [128, 16, 128], P(None, 'sub'), may hold values from -1.5 to 1.5
Outputs:
- gradient: float32 [1024, 4, 16, 128], P('fn', None, 'sub')
Inputs may be any that keep to these rules, and one draw needn't show every extreme that they name: `offsets`: Nondecreasing; each grid plane is the first plane of 1 to 15 boxes, both ends reached, on average 8; at most 46 boxes cover any plane (boxes wrap around the periodic wire), and some plane is covered by exactly 46.
All inputs are finite; a program needn't handle non-finite values.
Results may differ from a plain program's by a relative error of at most 0.0003.
Values sent between devices are 32-bit elements; how exact they have to be, the bound alone decides.
A program may use at most 64 MiB of HBM per device.

v0:
```python
import jax
import jax.numpy as jnp
from jax import lax
from jax.sharding import PartitionSpec as P

KMAX = 46
penalty = 0.5
highest = lax.Precision.HIGHEST


def sub_edges(cells):
    count = lax.axis_size("sub")
    up = [(i, i + 1) for i in range(count - 1)]
    down = [(i + 1, i) for i in range(count - 1)]
    rows = cells.shape[2]
    above = lax.ppermute(cells[:, :, rows - 1 : rows], "sub", up)
    below = lax.ppermute(cells[:, :, 0:1], "sub", down)
    return above, below


def sub_sum(part):
    count = lax.axis_size("sub")
    step = 1
    while step < count:
        part = part + lax.ppermute(part, "sub", [(i, i ^ step) for i in range(count)])
        step *= 2
    return part


def body(coeffs, offsets, potential):
    n = lax.axis_size("fn")
    e = lax.axis_index("fn")
    local, box, rows, depth = coeffs.shape
    planes = potential.shape[0]
    cells = rows * depth
    m = local // n
    h = -(-(KMAX - 1) // n)
    win = m + 2 * h
    volume = 1.0 / (box * 16 * 128)
    ext = jnp.concatenate([coeffs[local - h :], coeffs, coeffs[:h]], axis=0)
    send = jnp.stack([ext[m * k : m * k + win] for k in range(n)], axis=0)
    got = lax.all_to_all(send.reshape(n, win, box, cells), "fn", 0, 0, tiled=True)

    offs = offsets.reshape(local, n)
    offs = jnp.concatenate([offs[local - h :], offs, offs[:h]], axis=0)
    woff = lax.dynamic_slice_in_dim(offs, m * e, win, axis=0).T
    ooff = woff[:, h : h + m].reshape(-1)
    woff = woff.reshape(-1)

    own = got[:, h : h + m].reshape(local, box, rows, depth)
    above, below = sub_edges(own)
    phi_w = got.transpose(2, 0, 1, 3).reshape(box, n * win, cells)
    own_planes = (ooff[None, :] + jnp.arange(box, dtype=jnp.int32)[:, None]) % planes
    pick = (own_planes[:, :, None] == jnp.arange(planes, dtype=jnp.int32)).astype(jnp.float32)
    local_pot = lax.dot_general(
        pick.reshape(-1, planes), potential.reshape(planes, cells),
        (((1,), (0,)), ((), ())), precision=highest,
    ).reshape(box, local, rows, depth)

    o = own.transpose(1, 0, 2, 3)
    ab = above.transpose(1, 0, 2, 3)
    be = below.transpose(1, 0, 2, 3)
    yy = jnp.concatenate([ab, o, be], axis=2)
    zz = jnp.pad(o, ((0, 0), (0, 0), (0, 0), (1, 1)))
    beside = yy[:, :, 2:] + yy[:, :, :-2] + zz[..., 2:] + zz[..., :-2]
    u = -0.5 * (beside - 6.0 * o) + local_pot * o - penalty * o
    xx = jnp.pad(o, ((1, 1), (0, 0), (0, 0), (0, 0)))
    base = (u - 0.5 * (xx[2:] + xx[:-2])).reshape(box, local, cells)
    o = o.reshape(box, local, cells)
    u = u.reshape(box, local, cells)

    pair = jnp.stack([u, o]).reshape(2 * box * local, cells)
    gram = lax.dot_general(
        pair, phi_w.reshape(box * n * win, cells), (((1,), (1,)), ((), ())),
        precision=highest,
    ).reshape(2, box, local, box, n * win)
    diff = (ooff[:, None] - woff[None, :]) % planes
    masks = {k: diff == k % planes for k in range(1 - box, box)}
    total = jnp.zeros((local, n * win), jnp.float32)
    for p in range(box):
        for q in range(box):
            total = total + jnp.where(masks[q - p], gram[0, p, :, q], 0.0)
            if q + 1 < box:
                total = total - jnp.where(masks[q + 1 - p], 0.5 * gram[1, p, :, q], 0.0)
            if q >= 1:
                total = total - jnp.where(masks[q - 1 - p], 0.5 * gram[1, p, :, q], 0.0)
    band = sub_sum(volume * total)
    mix = jnp.stack(
        [
            jnp.stack([jnp.where(masks[q - p], band, 0.0) for q in range(box)], axis=1)
            for p in range(box)
        ]
    )
    update = base.reshape(box * local, cells) - lax.dot_general(
        mix.reshape(box * local, box * n * win), phi_w.reshape(box * n * win, cells),
        (((1,), (0,)), ((), ())), precision=highest,
    )
    back = update.reshape(box, n, m, cells).transpose(1, 2, 0, 3)
    back = lax.all_to_all(back, "fn", 0, 0, tiled=True)
    return back.reshape(local, box, rows, depth)


def solution(mesh):
    return jax.shard_map(
        body,
        mesh=mesh,
        in_specs=(P("fn", None, "sub", None), P(), P(None, "sub", None)),
        out_specs=P("fn", None, "sub", None),
        check_vma=False,
    )
```

profile of v0, /device:TPU:0, one launch (start us, length us, event | category | flops | bytes accessed | tf_op | source)
XLA Modules:
  0.0 134.1 jit_solution(9537893468355609020)
XLA Ops:
  0.0 0.8 fusion.110
  0.8 2.0 %pad_maximum_fusion.3 = (f32[28,4,4,128]{3,2,1,0:T(4,128)S(1)}, f32[28,4,4,128]{3,2,1,0:T(4,128)S(1)}, f32[28,4,4,128]{3,2,1,0:T(4,128)S(1)}, f32[28,4,4,128]{3,...) fusion(f32[6,4,4,128]{3,2,1,0:T(4,128)S(1)} %get-tuple-element., ...), kind=kLoop, calls=%fused_computation.35 | loop fusion | flops 114688 | bytes 4358144 | tf_op jit(solution)/shard_map/concatenate | solution.py:40
  2.9 0.1 stack.94
  3.0 0.1 stack.93
  3.1 0.1 stack.92
  3.3 0.1 stack.91
  3.4 0.1 stack.90
  3.6 0.1 stack.89
  3.7 0.1 stack.88
  3.9 0.1 stack.87
  4.0 0.7 constant_dynamic-update-slice_fusion.7
  4.7 0.7 constant_dynamic-update-slice_fusion.6
  5.4 0.7 constant_dynamic-update-slice_fusion.5
  6.1 0.7 constant_dynamic-update-slice_fusion.4
  6.8 0.7 constant_dynamic-update-slice_fusion.3
  7.5 0.7 constant_dynamic-update-slice_fusion.2
  8.2 0.7 constant_dynamic-update-slice_fusion.1
  8.9 0.7 constant_dynamic-update-slice_fusion
  9.6 7.4 %all-to-all-start = ((f32[8,28,4,512]{3,2,1,0:T(4,128)}), f32[8,28,4,512]{3,2,1,0:T(4,128)S(1)}, u32[]{:S(2)}, u32[]{:S(2)}) async-start(f32[8,28,4,512]{3,2,1,0:T(4,128)} %constant_dynamic-update-slice_fusion), calls=%async_computation | async-start | bytes 3670016 | tf_op jit(solution)/shard_map/all_to_all | solution.py:42
  17.6 42.1 %all-to-all-done = f32[8,28,4,512]{3,2,1,0:T(4,128)S(1)} async-done(((f32[8,28,4,512]{3,2,1,0:T(4,128)}), f32[8,28,4,512]{3,2,1,0:T(4,128)S(1)}, u32[]{:S(2)}, u32[]{:S(2)}) %all-to-all-start) | async-done | bytes 1835040 | tf_op jit(solution)/shard_map/all_to_all | solution.py:42
  59.7 0.1 slice.252
  59.8 1.6 %reshape.162 = f32[128,4,4,128]{3,2,1,0:T(4,128)} reshape(f32[8,16,4,512]{3,2,1,0:T(4,128)S(1)} %slice.252) | data formatting | bytes 2097152 | tf_op jit(solution)/shard_map/reshape | solution.py:50
  61.4 1.6 %copy.76 = f32[128,4,4,128]{0,3,2,1:T(8,128)S(1)} copy(f32[128,4,4,128]{3,2,1,0:T(4,128)} %reshape.162) | data formatting | bytes 2097152 | tf_op jit(solution)/shard_map/reshape | solution.py:50
  63.0 0.8 fusion.109
  63.8 1.3 collective-permute-start
  65.1 3.8 %collective-permute-start.1 = (f32[128,4,1,128]{0,3,2,1:T(8,128)}, f32[128,4,1,128]{0,3,2,1:T(8,128)}, u32[]{:S(2)}, u32[]{:S(2)}) collective-permute-start(f32[128,4,1,128]{0,3,2,1:T(8,128)} %get-tuple-element.8), channel_id=1, source_target_pairs={{0,1},{1,2},{2,3},{4,5},{5,6},{6,7},{8,9},{9,10},{10,11},{12,13},{... | collective-permute-start | bytes 786440 | tf_op jit(solution)/shard_map/ppermute | solution.py:16
  69.2 0.1 copy.82
  69.4 1.3 copy.85
  70.7 3.5 %fusion.18 = (f32[4,128,4,128]{1,3,2,0:T(8,128)}, f32[4,128,4,128]{1,3,2,0:T(8,128)}) fusion(f32[4,128,4,128]{1,3,2,0:T(8,128)S(1)} %bitcast.399, f32[4,128,128,1]{2,1,0,3:T(8,128)S(1)} %bitcast.406, s32[4,128]{1,0:T(4,128)S(1)} %add_select_fusion.1, f32[4,128,1,128]{1,3,2,0:T(8,128)} %bitcast.2, f32[4,128,1,128]{1,3,2,0:T(8,128)} %bitcast.1), kind=kOutput, calls=%fused_computation.23 | convolution fusion | flops 406650880 | bytes 3934208 | tf_op jit(solution)/shard_map/dot_general | solution.py:55
  74.2 2.6 %copy.84 = f32[1,4,128,512]{3,2,1,0:T(8,128)} copy(f32[1,4,128,512]{2,3,1,0:T(8,128)} %bitcast.403) | data formatting | bytes 2097152 | tf_op jit(solution)/shard_map/stack;reshape | solution.py:72
  76.8 7.9 %fusion = f32[2,4,128,4,224]{2,4,3,1,0:T(8,128)S(1)} fusion(f32[1,4,128,512]{3,2,1,0:T(8,128)S(1)} %copy-done, f32[1,4,128,512]{3,2,1,0:T(8,128)} %copy.84, f32[4,224,512,1,1]{2,0,1,4,3:T(4,128)S(1)} %bitcast.395), kind=kOutput, calls=%fused_computation.1 | convolution fusion | flops 5637668864 | bytes 7602176 | tf_op jit(solution)/shard_map/dot_general | solution.py:73
  84.7 0.6 fusion.27
  85.3 2.3 %collective-permute-start.2 = (f32[128,224]{0,1:T(8,128)S(1)}, f32[128,224]{0,1:T(8,128)S(1)}, u32[]{:S(2)}, u32[]{:S(2)}) collective-permute-start(f32[128,224]{0,1:T(8,128)S(1)} %fusion.27), channel_id=1, source_target_pairs={{0,1},{1,0},{2,3},{3,2},{4,5},{5,4},{6,7},{7,6},{8,9},{9,8},{10,11... | collective-permute-start | bytes 344072 | tf_op jit(solution)/shard_map/ppermute | solution.py:25
  87.6 1.0 collective-permute-done.2
  88.5 0.6 fusion.114
  89.1 2.8 %collective-permute-start.3 = (f32[128,224]{0,1:T(8,128)S(1)}, f32[128,224]{0,1:T(8,128)S(1)}, u32[]{:S(2)}, u32[]{:S(2)}) collective-permute-start(f32[128,224]{0,1:T(8,128)S(1)} %fusion.114), channel_id=1, source_target_pairs={{0,2},{1,3},{2,0},{3,1},{4,6},{5,7},{6,4},{7,5},{8,10},{9,11},{10,... | collective-permute-start | bytes 344072 | tf_op jit(solution)/shard_map/ppermute | solution.py:25
  91.9 1.9 %copy.88 = f32[4,8,28,512]{3,2,1,0:T(8,128)} copy(f32[4,8,28,512]{3,0,2,1:T(4,128)S(1)} %bitcast.396) | data formatting | bytes 3670016 | tf_op jit(solution)/shard_map/transpose | solution.py:52
  93.8 1.6 %reshape_reshape.8 = f32[896,512]{1,0:T(8,128)S(1)} reshape(f32[4,8,28,512]{3,2,1,0:T(8,128)} %copy.88) | data formatting | bytes 3670016 | tf_op jit(solution)/shard_map/reshape;reshape | solution.py:74
  95.5 1.6 %copy.83 = f32[4,128,4,128]{3,2,1,0:T(4,128)S(1)} copy(f32[4,128,4,128]{1,3,2,0:T(8,128)} %get-tuple-element.31) | data formatting | bytes 2097152 | tf_op jit(solution)/shard_map/sub | solution.py:68
  97.1 0.1 select_bitcast_fusion.3
  97.2 0.2 select_bitcast_fusion.4
  97.4 0.2 maximum_bitcast_fusion.2
  97.6 0.1 pad_maximum_fusion
  97.7 1.2 copy.87
  98.9 3.5 %fusion.7 = f32[512,512]{1,0:T(8,128)S(1)} fusion(f32[896,512]{1,0:T(8,128)S(1)} %reshape_reshape.8, f32[112,8,4,128]{3,2,1,0:T(4,128)S(1)} %bitcast.397, f32[64,8,4,128]{3,2,1,0:T(4,128)S(1)} %bitcast.401), kind=kOutput, calls=%fused_computation.11 | convolution fusion | flops 2818834432 | bytes 5767168 | tf_op jit(solution)/shard_map/dot_general | solution.py:94
  102.5 29.4 %all_to_all.10 = f32[8,16,4,512]{3,1,2,0:T(8,128)S(1)} all-to-all(f32[8,16,4,512]{3,1,2,0:T(8,128)S(1)} %bitcast.400), channel_id=1, replica_groups=mesh['fn'=8,'sub'=4] {'fn'}, dimensions={0} | all-to-all | bytes 2097152 | tf_op jit(solution)/shard_map/all_to_all | solution.py:99
  131.8 0.7 copy.101
  132.5 1.6 %reshape.163 = f32[128,4,4,128]{3,2,1,0:T(4,128)} reshape(f32[8,16,4,512]{3,2,1,0:T(4,128)S(1)} %copy.101) | data formatting | bytes 2097152 | tf_op jit(solution)/shard_map/reshape | solution.py:100
  (23 shorter events, 1.0 us)
Async XLA Ops:
  9.6 7.4 %copy-start.2 = (s32[1024]{0:T(1024)S(1)}, s32[1024]{0:T(1024)}, u32[]{:S(2)}) copy-start(s32[1024]{0:T(1024)} %param.4) | copy-start | bytes 12292
  9.6 50.0 %all-to-all-start = ((f32[8,28,4,512]{3,2,1,0:T(4,128)}), f32[8,28,4,512]{3,2,1,0:T(4,128)S(1)}, u32[]{:S(2)}, u32[]{:S(2)}) async-start(f32[8,28,4,512]{3,2,1,0:T(4,128)} %constant_dynamic-update-slice_fusion), calls=%async_computation | async-start | bytes 3670016 | tf_op jit(solution)/shard_map/all_to_all | solution.py:42
  61.4 7.8 %copy-start.1 = (f32[128,4,128]{2,1,0:T(4,128)S(1)}, f32[128,4,128]{2,1,0:T(4,128)}, u32[]{:S(2)}) copy-start(f32[128,4,128]{2,1,0:T(4,128)} %param.5) | copy-start | bytes 786436
  63.8 6.9 %collective-permute-start = (f32[128,4,1,128]{0,3,2,1:T(8,128)}, f32[128,4,1,128]{0,3,2,1:T(8,128)}, u32[]{:S(2)}, u32[]{:S(2)}) collective-permute-start(f32[128,4,1,128]{0,3,2,1:T(8,128)} %get-tuple-element.7), channel_id=1, source_target_pairs={{1,0},{2,1},{3,2},{5,4},{6,5},{7,6},{9,8},{10,9},{11,10},{13,12},{... | collective-permute-start | bytes 786440 | tf_op jit(solution)/shard_map/ppermute | solution.py:17
  65.1 5.6 %collective-permute-start.1 = (f32[128,4,1,128]{0,3,2,1:T(8,128)}, f32[128,4,1,128]{0,3,2,1:T(8,128)}, u32[]{:S(2)}, u32[]{:S(2)}) collective-permute-start(f32[128,4,1,128]{0,3,2,1:T(8,128)} %get-tuple-element.8), channel_id=1, source_target_pairs={{0,1},{1,2},{2,3},{4,5},{5,6},{6,7},{8,9},{9,10},{10,11},{12,13},{... | collective-permute-start | bytes 786440 | tf_op jit(solution)/shard_map/ppermute | solution.py:16
  74.2 2.6 %copy-start = (f32[1,4,128,512]{3,2,1,0:T(8,128)S(1)}, f32[1,4,128,512]{3,2,1,0:T(8,128)}, u32[]{:S(2)}) copy-start(f32[1,4,128,512]{3,2,1,0:T(8,128)} %copy.85) | copy-start | bytes 3145732
  85.3 3.2 %collective-permute-start.2 = (f32[128,224]{0,1:T(8,128)S(1)}, f32[128,224]{0,1:T(8,128)S(1)}, u32[]{:S(2)}, u32[]{:S(2)}) collective-permute-start(f32[128,224]{0,1:T(8,128)S(1)} %fusion.27), channel_id=1, source_target_pairs={{0,1},{1,0},{2,3},{3,2},{4,5},{5,4},{6,7},{7,6},{8,9},{9,8},{10,11... | collective-permute-start | bytes 344072 | tf_op jit(solution)/shard_map/ppermute | solution.py:25
  89.1 8.0 %collective-permute-start.3 = (f32[128,224]{0,1:T(8,128)S(1)}, f32[128,224]{0,1:T(8,128)S(1)}, u32[]{:S(2)}, u32[]{:S(2)}) collective-permute-start(f32[128,224]{0,1:T(8,128)S(1)} %fusion.114), channel_id=1, source_target_pairs={{0,2},{1,3},{2,0},{3,1},{4,6},{5,7},{6,4},{7,5},{8,10},{9,11},{10,... | collective-permute-start | bytes 344072 | tf_op jit(solution)/shard_map/ppermute | solution.py:25
where the time goes:
time: 135 us; the launch traced here: 134 us
  waiting for transfers between devices  43.1 us (32%)
  blocking collectives  29.4 us (22%)
  local copies, waits for them, and re-layouts  25.2 us (19%)
  starting transfers between devices  17.5 us (13%)
  matrix products  14.9 us (11%)
  other arithmetic  3.85 us (3%)
    all_to_all x1, waiting for transfers between devices, body(): lax.all_to_all(send.reshape(n, win, box, cells), 'fn', 0, 0, tiled=True)  42.1 us
    all_to_all x1, blocking collectives, body(): back = lax.all_to_all(back, 'fn', 0, 0, tiled=True)  29.4 us
    dot_general x1, matrix products, body(): lax.dot_general(pair, phi_w.reshape(box * n * win, cells), (((1,), (1,)),...  7.87 us
    all_to_all x1, starting transfers between devices, body(): lax.all_to_all(send.reshape(n, win, box, cells), 'fn', 0, 0, tiled=True)  7.41 us
    ppermute x2, starting transfers between devices, sub_sum(): lax.ppermute(part, 'sub', [(i, i ^ step) for i in range(count)])  5.07 us
    unnamed x14, local copies, waits for them, and re-layouts  4.98 us
    another operation x2, local copies, waits for them, and re-layouts, body(): pair = jnp.stack([u, o]).reshape(2 * box * local, cells)  3.94 us
    ppermute x1, starting transfers between devices, sub_edges(): above = lax.ppermute(cells[:, :, rows - 1:rows], 'sub', up)  3.77 us
  transfers between devices with their start and end apart: 5, of which 2 were waited for; matrix products, arithmetic and copies ran while one was open for 6% of the time, Pallas kernels for 0%

commit v1 on v0

v1 whole, which is shorter than its diff:
```python
import functools

import jax
import jax.numpy as jnp
from jax import lax
from jax.experimental import pallas as pl
from jax.experimental.pallas import tpu as pltpu
from jax.sharding import PartitionSpec as P

KMAX = 46
penalty = 0.5
VMEM = pl.BlockSpec(memory_space=pltpu.VMEM)


def split(x):
    hi = x.astype(jnp.bfloat16)
    return hi, (x - hi.astype(jnp.float32)).astype(jnp.bfloat16)


def dot_t(a, b):
    return lax.dot_general(a, b, (((1,), (1,)), ((), ())), preferred_element_type=jnp.float32)


def dot(a, b):
    return jnp.dot(a, b, preferred_element_type=jnp.float32)


def gram_kernel(
    box, rows, planes, volume,
    own_ref, left_ref, right_ref, above_ref, below_ref, pot_ref, ooff_ref, woff_ref,
    total_ref, base_ref, right_hand_ref,
    hi_ref, lo_ref,
):
    per = box * rows
    local = own_ref.shape[0] // per
    side = left_ref.shape[0] // per
    win = local + 2 * side
    depth = own_ref.shape[1]
    cells = rows * depth
    lane = lax.broadcasted_iota(jnp.int32, (local, depth), 1)
    plane_ids = lax.broadcasted_iota(jnp.int32, (local, planes), 1)
    ooff = ooff_ref[...]

    def piece(p, r):
        return own_ref[pl.ds(p * rows + r, local, stride=per), :]

    for p in range(box):
        wanted = ooff + p
        wanted = jnp.where(wanted >= planes, wanted - planes, wanted)
        pick = (plane_ids == wanted).astype(jnp.float32).astype(jnp.bfloat16)
        for r in range(rows):
            cols = pl.ds(r * depth, depth)
            o = piece(p, r)
            up = piece(p, r - 1) if r > 0 else above_ref[pl.ds(p, local, stride=box), :]
            down = piece(p, r + 1) if r < rows - 1 else below_ref[pl.ds(p, local, stride=box), :]
            zl = jnp.where(lane == 0, 0.0, pltpu.roll(o, 1, axis=1))
            zr = jnp.where(lane == depth - 1, 0.0, pltpu.roll(o, depth - 1, axis=1))
            pot_hi, pot_lo = split(pot_ref[pl.ds(r, planes, stride=rows), :])
            pot = dot(pick, pot_hi) + dot(pick, pot_lo)
            u = -0.5 * (up + down + zl + zr - 6.0 * o) + pot * o - penalty * o
            base = u
            if p > 0:
                base = base - 0.5 * piece(p - 1, r)
            if p < box - 1:
                base = base - 0.5 * piece(p + 1, r)
            base_ref[pl.ds(p * local, local), cols] = base
            u_hi, u_lo = split(u)
            hi_ref[pl.ds(p * local, local), cols] = u_hi
            lo_ref[pl.ds(p * local, local), cols] = u_lo
            o_hi, o_lo = split(o)
            hi_ref[pl.ds((box + p) * local, local), cols] = o_hi
            lo_ref[pl.ds((box + p) * local, local), cols] = o_lo
            low = pl.ds(cells + r * depth, depth)
            right_hand_ref[pl.ds(p * win + side, local), cols] = o_hi
            right_hand_ref[pl.ds(p * win + side, local), low] = o_lo
            for ref, at in ((left_ref, 0), (right_ref, side + local)):
                x_hi, x_lo = split(ref[pl.ds(p * rows + r, side, stride=per), :])
                right_hand_ref[pl.ds(p * win + at, side), cols] = x_hi
                right_hand_ref[pl.ds(p * win + at, side), low] = x_lo

    diff = ooff - woff_ref[...]
    masks = {}
    for k in range(1 - box, box):
        masks[k] = (diff == k) | (diff == k + planes) | (diff == k - planes)
    total = jnp.zeros((local, win), jnp.float32)
    for q in range(box):
        r_hi = right_hand_ref[pl.ds(q * win, win), pl.ds(0, cells)]
        r_lo = right_hand_ref[pl.ds(q * win, win), pl.ds(cells, cells)]
        for p in range(2 * box):
            at = pl.ds(p * local, local)
            l_hi, l_lo = hi_ref[at, :], lo_ref[at, :]
            gram = dot_t(l_hi, r_hi) + dot_t(l_hi, r_lo) + dot_t(l_lo, r_hi)
            if p < box:
                total = total + jnp.where(masks[q - p], gram, 0.0)
                continue
            if q + 1 < box:
                total = total - jnp.where(masks[q + 1 - p + box], 0.5 * gram, 0.0)
            if q >= 1:
                total = total - jnp.where(masks[q - 1 - p + box], 0.5 * gram, 0.0)
    total_ref[...] = volume * total


def mix_kernel(
    box, rows, planes,
    band_ref, base_ref, right_hand_ref, ooff_ref, woff_ref,
    out_ref,
    hi_ref, lo_ref,
):
    per = box * rows
    local, win = band_ref.shape
    cells = base_ref.shape[1]
    depth = cells // rows
    diff = ooff_ref[...] - woff_ref[...]
    b_hi, b_lo = split(band_ref[...])
    b_hi = b_hi.astype(jnp.float32)
    b_lo = b_lo.astype(jnp.float32)
    picked = {}
    for k in range(1 - box, box):
        mask = (diff == k) | (diff == k + planes) | (diff == k - planes)
        picked[k] = (
            jnp.where(mask, b_hi, 0.0).astype(jnp.bfloat16),
            jnp.where(mask, b_lo, 0.0).astype(jnp.bfloat16),
        )
    for p in range(box):
        update = base_ref[pl.ds(p * local, local), :]
        for q in range(box):
            r_hi = right_hand_ref[pl.ds(q * win, win), pl.ds(0, cells)]
            r_lo = right_hand_ref[pl.ds(q * win, win), pl.ds(cells, cells)]
            a_hi, a_lo = picked[q - p]
            update = update - (dot(a_hi, r_hi) + dot(a_hi, r_lo) + dot(a_lo, r_hi))
        for r in range(rows):
            out_ref[pl.ds(p * rows + r, local, stride=per), :] = update[:, r * depth : (r + 1) * depth]


def sub_edges(cells):
    count = lax.axis_size("sub")
    up = [(i, i + 1) for i in range(count - 1)]
    down = [(i + 1, i) for i in range(count - 1)]
    rows = cells.shape[2]
    above = lax.ppermute(cells[:, :, rows - 1], "sub", up)
    below = lax.ppermute(cells[:, :, 0], "sub", down)
    return above, below


def sub_sum(part):
    count = lax.axis_size("sub")
    step = 1
    while step < count:
        part = part + lax.ppermute(part, "sub", [(i, i ^ step) for i in range(count)])
        step *= 2
    return part


def body(coeffs, offsets, potential):
    n = lax.axis_size("fn")
    e = lax.axis_index("fn")
    local, box, rows, depth = coeffs.shape
    planes = potential.shape[0]
    cells = rows * depth
    m = local // n
    h = -(-(KMAX - 1) // n)
    side = h * n
    win = local + 2 * side
    volume = 1.0 / (box * 16 * 128)

    got = lax.all_to_all(coeffs.reshape(n, m, box, rows, depth), "fn", 0, 0, tiled=True)
    left = lax.ppermute(got[:, m - h :], "fn", [(i, (i + 1) % n) for i in range(n)])
    right = lax.ppermute(got[:, :h], "fn", [((i + 1) % n, i) for i in range(n)])
    above, below = sub_edges(got.reshape(local, box, rows, depth))

    offs = offsets.reshape(local, n)
    offs = jnp.concatenate([offs[local - h :], offs, offs[:h]], axis=0)
    woff = lax.dynamic_slice_in_dim(offs, m * e, m + 2 * h, axis=0)
    ooff = woff[h : h + m].T.reshape(local, 1)
    woff = jnp.concatenate(
        [woff[:h].T.reshape(1, side), ooff.reshape(1, local), woff[h + m :].T.reshape(1, side)],
        axis=1,
    )

    total, base, right_hand = pl.pallas_call(
        functools.partial(gram_kernel, box, rows, planes, volume),
        out_shape=(
            jax.ShapeDtypeStruct((local, win), jnp.float32),
            jax.ShapeDtypeStruct((box * local, cells), jnp.float32),
            jax.ShapeDtypeStruct((box * win, 2 * cells), jnp.bfloat16),
        ),
        in_specs=[VMEM] * 8,
        out_specs=(VMEM,) * 3,
        scratch_shapes=[pltpu.VMEM((2 * box * local, cells), jnp.bfloat16)] * 2,
        name="gram",
    )(
        got.reshape(-1, depth), left.reshape(-1, depth), right.reshape(-1, depth),
        above.reshape(-1, depth), below.reshape(-1, depth),
        potential.reshape(-1, depth), ooff, woff,
    )
    band = sub_sum(total)
    update = pl.pallas_call(
        functools.partial(mix_kernel, box, rows, planes),
        out_shape=jax.ShapeDtypeStruct((local * box * rows, depth), jnp.float32),
        in_specs=[VMEM] * 5,
        out_specs=VMEM,
        scratch_shapes=[pltpu.VMEM((8, 128), jnp.float32)] * 2,
        name="mix",
    )(band, base, right_hand, ooff, woff)
    back = lax.all_to_all(update.reshape(n, m, box, rows, depth), "fn", 0, 0, tiled=True)
    return back.reshape(local, box, rows, depth)


def solution(mesh):
    return jax.shard_map(
        body,
        mesh=mesh,
        in_specs=(P("fn", None, "sub", None), P(), P(None, "sub", None)),
        out_specs=P("fn", None, "sub", None),
        check_vma=False,
    )
```

time: 135 us -> 109 us (0.81)
  local copies, waits for them, and re-layouts: 25.2 us -> 3.72 us
  Pallas kernels: 0 us -> 16.1 us
  matrix products: 14.9 us -> 0 us
  waiting for transfers between devices: 43.1 us -> 40.3 us
  starting transfers between devices: 17.5 us -> 15.7 us
  other arithmetic: 3.85 us -> 2.36 us
    all_to_all x1, waiting for transfers between devices: 42.1 us -> 24.2 us  [body(): lax.all_to_all(coeffs.reshape(n, m, box, rows, depth), 'fn', 0, 0, tiled=...]
    pallas_call x0 -> x2, Pallas kernels: none -> 16.1 us  [the longest x1 11.1 us: body(): pl.pallas_call(functools.partial(gram_kernel, box, rows, planes, volume),...]
    dot_general x3 -> x0, matrix products: 14.9 us -> none  [the longest x1 7.87 us: body(): lax.dot_general(pair, phi_w.reshape(box * n * win, cells), (((1,), (1,)),...]
    ppermute x2 -> x4, waiting for transfers between devices: 0.01 us -> 10.5 us  [the longest x1 10.1 us: body(): right = lax.ppermute(got[:, :h], 'fn', [((i + 1) % n, i) for i in range(n)])]
    another operation x13 -> x1, local copies, waits for them, and re-layouts: 8.53 us -> 0.08 us  [body(): ooff.reshape(1, local)]
    reshape x5 -> x3, local copies, waits for them, and re-layouts: 5.53 us -> 0.89 us  [the longest x1 0.73 us: body(): ooff = woff[h:h + m].T.reshape(local, 1)]
    ppermute x2, waiting for transfers between devices: 0.97 us -> 5.57 us  [sub_sum(): lax.ppermute(part, 'sub', [(i, i ^ step) for i in range(count)])]
    ppermute x2, starting transfers between devices: 5.07 us -> 1.61 us  [sub_sum(): lax.ppermute(part, 'sub', [(i, i ^ step) for i in range(count)])]
  transfers between devices with their start and end apart: 5 -> 7, of which waited for: 2 -> 6; matrix products, arithmetic and copies ran while one was open for 6% -> 3% of each run, Pallas kernels for 0% -> 0%
where the time goes in v1:
time: 109 us; the launch traced here: 108 us
  waiting for transfers between devices  40.3 us (37%)
  blocking collectives  30 us (28%)
  Pallas kernels  16.1 us (15%)
  starting transfers between devices  15.7 us (14%)
  local copies, waits for them, and re-layouts  3.72 us (3%)
  other arithmetic  2.36 us (2%)
    all_to_all x1, blocking collectives, body(): lax.all_to_all(update.reshape(n, m, box, rows, depth), 'fn', 0, 0, tiled=...  30 us
    all_to_all x1, waiting for transfers between devices, body(): lax.all_to_all(coeffs.reshape(n, m, box, rows, depth), 'fn', 0, 0, tiled=...  24.2 us
    pallas_call x1, Pallas kernels, body(): pl.pallas_call(functools.partial(gram_kernel, box, rows, planes, volume),...  11.1 us
    ppermute x1, waiting for transfers between devices, body(): right = lax.ppermute(got[:, :h], 'fn', [((i + 1) % n, i) for i in range(n)])  10.1 us
    all_to_all x1, starting transfers between devices, body(): lax.all_to_all(coeffs.reshape(n, m, box, rows, depth), 'fn', 0, 0, tiled=...  7.41 us
    ppermute x2, waiting for transfers between devices, sub_sum(): lax.ppermute(part, 'sub', [(i, i ^ step) for i in range(count)])  5.57 us
    pallas_call x1, Pallas kernels, body(): pl.pallas_call(functools.partial(mix_kernel, box, rows, planes), out_shap...  5.04 us
    ppermute x1, starting transfers between devices, sub_edges(): above = lax.ppermute(cells[:, :, rows - 1], 'sub', up)  3.05 us
  transfers between devices with their start and end apart: 7, of which 6 were waited for; matrix products, arithmetic and copies ran while one was open for 3% of the time, Pallas kernels for 0%

profile of v1, /device:TPU:0, one launch (start us, length us, event | category | flops | bytes accessed | tf_op | source)
XLA Modules:
  0.0 108.3 jit_solution(13491304986404252328)
XLA Ops:
  0.0 0.0 copy-start.5
  0.0 7.4 %all-to-all-start = ((f32[8,16,4,4,128]{4,3,2,1,0:T(4,128)}), f32[8,16,4,4,128]{4,3,2,1,0:T(4,128)S(1)}, u32[]{:S(2)}, u32[]{:S(2)}) async-start(f32[8,16,4,4,128]{4,3,2,1,0:T(4,128)} %bitcast.24), calls=%async_computation | async-start | bytes 2097152 | tf_op jit(solution)/shard_map/all_to_all | solution.py:166
  7.4 0.0 copy-done.5
  7.4 0.1 reshape.68
  7.5 0.1 fusion.3
  7.6 0.1 slice.56
  7.7 0.1 copy.19
  7.7 0.1 slice.54
  7.8 0.1 copy.17
  8.0 0.1 fusion.1
  8.1 0.1 slice_bitcast_fusion.4
  8.1 0.1 reshape_reshape.3
  8.2 0.7 reshape.74.ooff_ref
  8.9 24.2 %all-to-all-done = f32[8,16,4,4,128]{4,3,2,1,0:T(4,128)S(1)} async-done(((f32[8,16,4,4,128]{4,3,2,1,0:T(4,128)}), f32[8,16,4,4,128]{4,3,2,1,0:T(4,128)S(1)}, u32[]{:S(2)}, u32[]{:S(2)}) %all-to-all-start) | async-done | bytes 1048608 | tf_op jit(solution)/shard_map/all_to_all | solution.py:166
  33.2 0.0 copy-start
  33.2 0.1 fusion.2
  33.2 2.4 %collective-permute-start.1 = (f32[8,6,4,4,128]{4,3,2,1,0:T(4,128)S(1)}, f32[8,6,4,4,128]{4,3,2,1,0:T(4,128)S(1)}, u32[]{:S(2)}, u32[]{:S(2)}) collective-permute-start(f32[8,6,4,4,128]{4,3,2,1,0:T(4,128)S(1)} %get-tuple-element.13), channel_id=1, source_target_pairs={{4,0},{8,4},{12,8},{16,12},{20,16},{24,20},{28,24},{0,28},{5,1},{9... | collective-permute-start | bytes 1179656 | tf_op jit(solution)/shard_map/ppermute | solution.py:168
  35.6 0.0 collective-permute-start
  35.6 0.3 copy.16
  35.9 0.0 copy-done
  35.9 1.3 %collective-permute-start.3 = (f32[128,4,128]{2,1,0:T(4,128)S(1)}, f32[128,4,128]{2,1,0:T(4,128)S(1)}, u32[]{:S(2)}, u32[]{:S(2)}) collective-permute-start(f32[128,4,128]{2,1,0:T(4,128)S(1)} %get-tuple-element.11), channel_id=1, source_target_pairs={{1,0},{2,1},{3,2},{5,4},{6,5},{7,6},{9,8},{10,9},{11,10},{13,12},{... | collective-permute-start | bytes 786440 | tf_op jit(solution)/shard_map/ppermute | solution.py:141
  37.2 3.0 %collective-permute-start.2 = (f32[128,4,128]{2,1,0:T(4,128)S(1)}, f32[128,4,128]{2,1,0:T(4,128)S(1)}, u32[]{:S(2)}, u32[]{:S(2)}) collective-permute-start(f32[128,4,128]{2,1,0:T(4,128)S(1)} %get-tuple-element.12), channel_id=1, source_target_pairs={{0,1},{1,2},{2,3},{4,5},{5,6},{6,7},{8,9},{9,10},{10,11},{12,13},{... | collective-permute-start | bytes 786440 | tf_op jit(solution)/shard_map/ppermute | solution.py:140
  40.3 0.1 slice_bitcast_fusion.3
  40.4 0.1 reshape.70
  40.5 0.1 reshape.71
  40.5 0.7 pad_add_fusion.woff_ref
  41.2 0.0 collective-permute-done.3
  41.2 0.0 copy-start.3
  41.2 0.2 collective-permute-done.2
  41.4 0.0 copy-start.4
  41.4 10.1 %collective-permute-done.1 = f32[8,6,4,4,128]{4,3,2,1,0:T(4,128)S(1)} collective-permute-done((f32[8,6,4,4,128]{4,3,2,1,0:T(4,128)S(1)}, f32[8,6,4,4,128]{4,3,2,1,0:T(4,128)S(1)}, u32[]{:S(2)}, u32[]{:S(2)}) %collective-permute-start.1) | collective-permute-done | bytes 393248 | tf_op jit(solution)/shard_map/ppermute | solution.py:168
  51.5 0.0 copy-start.1
  51.5 0.2 collective-permute-done
  51.7 0.0 copy-start.2
  51.7 0.0 copy-done.3
  51.7 0.0 copy-done.4
  51.7 0.6 copy-done.1
  52.3 0.1 copy-done.2
  52.4 11.1 %gram.1 = (f32[128,224]{1,0:T(8,128)}, f32[512,512]{1,0:T(8,128)}, bf16[896,1024]{1,0:T(8,128)(2,1)}) custom-call(f32[2048,128]{1,0:T(8,128)} %bitcast.20, f32[768,128]{1,0:T(8,128)} %bitcast.26, f32[768,128]{1,0:T(8,128)} %bitcast.25, f32[512,128]{1,0:T(8,128)} %bitcast.29, f32[512,128]{1,0:T(8,128)} %bitcast.28, f32[512,128]{1,0:T(8,128)} %bitcast.27, ...), custom_call_target="tpu_custom_call" | custom-call | tf_op jit(solution)/shard_map/gram/pallas_call | solution.py:180
  63.5 0.0 collective-permute-start.4
  63.6 1.5 %collective-permute-done.4 = f32[128,224]{1,0:T(8,128)S(1)} collective-permute-done((f32[128,224]{1,0:T(8,128)}, f32[128,224]{1,0:T(8,128)S(1)}, u32[]{:S(2)}, u32[]{:S(2)}) %collective-permute-start.4) | collective-permute-done | bytes 114720 | tf_op jit(solution)/shard_map/ppermute | solution.py:149
  65.1 0.9 add.10
  66.0 1.6 %collective-permute-start.5 = (f32[128,224]{1,0:T(8,128)S(1)}, f32[128,224]{1,0:T(8,128)S(1)}, u32[]{:S(2)}, u32[]{:S(2)}) collective-permute-start(f32[128,224]{1,0:T(8,128)S(1)} %add.10), channel_id=1, source_target_pairs={{0,2},{1,3},{2,0},{3,1},{4,6},{5,7},{6,4},{7,5},{8,10},{9,11},{10,... | collective-permute-start | bytes 344072 | tf_op jit(solution)/shard_map/ppermute | solution.py:149
  67.6 4.0 %collective-permute-done.5 = f32[128,224]{1,0:T(8,128)S(1)} collective-permute-done((f32[128,224]{1,0:T(8,128)S(1)}, f32[128,224]{1,0:T(8,128)S(1)}, u32[]{:S(2)}, u32[]{:S(2)}) %collective-permute-start.5) | collective-permute-done | bytes 114720 | tf_op jit(solution)/shard_map/ppermute | solution.py:149
  71.6 0.7 add.11.band_ref
  72.3 5.0 %mix.1 = f32[2048,128]{1,0:T(8,128)} custom-call(f32[128,224]{1,0:T(8,128)} %add.11.band_ref, f32[512,512]{1,0:T(8,128)} %get-tuple-element.9.base_ref, bf16[896,1024]{1,0:T(8,128)(2,1)} %get-tuple-element.10.right_hand_ref, s32[128,1]{1,0:T(8,128)} %reshape.74.ooff_ref, s32[1,224]{1,0:T(1,128)} %pad_add_fusion.woff_ref), custom_call_target="tpu_custom_call" | custom-call | tf_op jit(solution)/shard_map/mix/pallas_call | solution.py:197
  77.3 30.0 %all_to_all.10 = f32[8,16,4,4,128]{4,3,2,1,0:T(4,128)S(1)} all-to-all(f32[8,16,4,4,128]{4,3,2,1,0:T(4,128)} %bitcast.21), channel_id=1, replica_groups=mesh['fn'=8,'sub'=4] {'fn'}, dimensions={0} | all-to-all | bytes 2097152 | tf_op jit(solution)/shard_map/all_to_all | solution.py:205
  107.3 1.0 copy.23
  (2 shorter events, 0.1 us)
Async XLA Ops:
  0.0 7.4 %copy-start.5 = (s32[1024]{0:T(1024)S(1)}, s32[1024]{0:T(1024)}, u32[]{:S(2)}) copy-start(s32[1024]{0:T(1024)} %param.4) | copy-start | bytes 12292
  0.0 33.2 %all-to-all-start = ((f32[8,16,4,4,128]{4,3,2,1,0:T(4,128)}), f32[8,16,4,4,128]{4,3,2,1,0:T(4,128)S(1)}, u32[]{:S(2)}, u32[]{:S(2)}) async-start(f32[8,16,4,4,128]{4,3,2,1,0:T(4,128)} %bitcast.24), calls=%async_computation | async-start | bytes 2097152 | tf_op jit(solution)/shard_map/all_to_all | solution.py:166
  33.2 2.7 %copy-start = (f32[8,16,4,4,128]{4,3,2,1,0:T(4,128)}, f32[8,16,4,4,128]{4,3,2,1,0:T(4,128)S(1)}, u32[]{:S(2)}) copy-start(f32[8,16,4,4,128]{4,3,2,1,0:T(4,128)S(1)} %all-to-all-done) | copy-start | bytes 3145732
  33.2 18.3 %collective-permute-start.1 = (f32[8,6,4,4,128]{4,3,2,1,0:T(4,128)S(1)}, f32[8,6,4,4,128]{4,3,2,1,0:T(4,128)S(1)}, u32[]{:S(2)}, u32[]{:S(2)}) collective-permute-start(f32[8,6,4,4,128]{4,3,2,1,0:T(4,128)S(1)} %get-tuple-element.13), channel_id=1, source_target_pairs={{4,0},{8,4},{12,8},{16,12},{20,16},{24,20},{28,24},{0,28},{5,1},{9... | collective-permute-start | bytes 1179656 | tf_op jit(solution)/shard_map/ppermute | solution.py:168
  35.6 16.1 %collective-permute-start = (f32[8,6,4,4,128]{4,3,2,1,0:T(4,128)S(1)}, f32[8,6,4,4,128]{4,3,2,1,0:T(4,128)S(1)}, u32[]{:S(2)}, u32[]{:S(2)}) collective-permute-start(f32[8,6,4,4,128]{4,3,2,1,0:T(4,128)S(1)} %get-tuple-element.14), channel_id=1, source_target_pairs={{0,4},{4,8},{8,12},{12,16},{16,20},{20,24},{24,28},{28,0},{1,5},{5... | collective-permute-start | bytes 1179656 | tf_op jit(solution)/shard_map/ppermute | solution.py:167
  35.9 5.3 %collective-permute-start.3 = (f32[128,4,128]{2,1,0:T(4,128)S(1)}, f32[128,4,128]{2,1,0:T(4,128)S(1)}, u32[]{:S(2)}, u32[]{:S(2)}) collective-permute-start(f32[128,4,128]{2,1,0:T(4,128)S(1)} %get-tuple-element.11), channel_id=1, source_target_pairs={{1,0},{2,1},{3,2},{5,4},{6,5},{7,6},{9,8},{10,9},{11,10},{13,12},{... | collective-permute-start | bytes 786440 | tf_op jit(solution)/shard_map/ppermute | solution.py:141
  37.2 4.2 %collective-permute-start.2 = (f32[128,4,128]{2,1,0:T(4,128)S(1)}, f32[128,4,128]{2,1,0:T(4,128)S(1)}, u32[]{:S(2)}, u32[]{:S(2)}) collective-permute-start(f32[128,4,128]{2,1,0:T(4,128)S(1)} %get-tuple-element.12), channel_id=1, source_target_pairs={{0,1},{1,2},{2,3},{4,5},{5,6},{6,7},{8,9},{9,10},{10,11},{12,13},{... | collective-permute-start | bytes 786440 | tf_op jit(solution)/shard_map/ppermute | solution.py:140
  41.2 10.5 %copy-start.3 = (f32[128,4,128]{2,1,0:T(4,128)}, f32[128,4,128]{2,1,0:T(4,128)S(1)}, u32[]{:S(2)}) copy-start(f32[128,4,128]{2,1,0:T(4,128)S(1)} %collective-permute-done.3) | copy-start | bytes 786436
  41.4 10.3 %copy-start.4 = (f32[128,4,128]{2,1,0:T(4,128)}, f32[128,4,128]{2,1,0:T(4,128)S(1)}, u32[]{:S(2)}) copy-start(f32[128,4,128]{2,1,0:T(4,128)S(1)} %collective-permute-done.2) | copy-start | bytes 786436
  51.5 0.7 copy-start.1
  51.7 0.7 copy-start.2
  63.5 1.6 %collective-permute-start.4 = (f32[128,224]{1,0:T(8,128)}, f32[128,224]{1,0:T(8,128)S(1)}, u32[]{:S(2)}, u32[]{:S(2)}) collective-permute-start(f32[128,224]{1,0:T(8,128)} %get-tuple-element.8), channel_id=1, source_target_pairs={{0,1},{1,0},{2,3},{3,2},{4,5},{5,4},{6,7},{7,6},{8,9},{9,8},{10,11... | collective-permute-start | bytes 344072 | tf_op jit(solution)/shard_map/ppermute | solution.py:149
  66.0 5.6 %collective-permute-start.5 = (f32[128,224]{1,0:T(8,128)S(1)}, f32[128,224]{1,0:T(8,128)S(1)}, u32[]{:S(2)}, u32[]{:S(2)}) collective-permute-start(f32[128,224]{1,0:T(8,128)S(1)} %add.10), channel_id=1, source_target_pairs={{0,2},{1,3},{2,0},{3,1},{4,6},{5,7},{6,4},{7,5},{8,10},{9,11},{10,... | collective-permute-start | bytes 344072 | tf_op jit(solution)/shard_map/ppermute | solution.py:149

commit v2 on v1

v2 whole, which is shorter than its diff:
```python
import functools

import jax
import jax.numpy as jnp
from jax import lax
from jax.experimental import pallas as pl
from jax.experimental.pallas import tpu as pltpu
from jax.sharding import PartitionSpec as P

KMAX = 46
penalty = 0.5
VMEM = pl.BlockSpec(memory_space=pltpu.VMEM)


def split(x):
    hi = x.astype(jnp.bfloat16)
    return hi, (x - hi.astype(jnp.float32)).astype(jnp.bfloat16)


def dot_t(a, b):
    return lax.dot_general(a, b, (((1,), (1,)), ((), ())), preferred_element_type=jnp.float32)


def dot(a, b):
    return jnp.dot(a, b, preferred_element_type=jnp.float32)


def dot3_t(l_hi, l_lo, r_hi, r_lo):
    return dot_t(l_hi, r_hi) + dot_t(l_hi, r_lo) + dot_t(l_lo, r_hi)


def delta_masks(box, planes, diff):
    return {
        k: (diff == k) | (diff == k + planes) | (diff == k - planes) for k in range(1 - box, box)
    }


def masked_sum(box, planes, diff, hi_ref, lo_ref, r_hi_ref, r_lo_ref, first):
    local, width = diff.shape
    masks = delta_masks(box, planes, diff)
    total = jnp.zeros((local, width), jnp.float32)
    for q0 in range(0, box, 2):
        at = pl.ds(first + q0 * width, 2 * width)
        grams = dot3_t(hi_ref[...], lo_ref[...], r_hi_ref[at, :], r_lo_ref[at, :])
        for q in (q0, q0 + 1):
            for p in range(box):
                cols = slice((q - q0) * width, (q - q0 + 1) * width)
                plain = grams[p * local : (p + 1) * local, cols]
                beside = 0.5 * grams[(box + p) * local : (box + p + 1) * local, cols]
                total = total + jnp.where(masks[q - p], plain, 0.0)
                if q + 1 < box:
                    total = total - jnp.where(masks[q + 1 - p], beside, 0.0) if q + 1 - p < box else total
                if q >= 1:
                    total = total - jnp.where(masks[q - 1 - p], beside, 0.0) if q - 1 - p > -box else total
    return total


def own_kernel(
    box, rows, planes,
    own_ref, above_ref, below_ref, pot_ref, ooff_ref, row_ref,
    total_ref, base_ref, hi_ref, lo_ref,
):
    per = box * rows
    local = own_ref.shape[0] // per
    depth = own_ref.shape[1]
    lane = lax.broadcasted_iota(jnp.int32, (local, depth), 1)
    plane_ids = lax.broadcasted_iota(jnp.int32, (local, planes), 1)
    ooff = ooff_ref[...]

    def piece(p, r):
        return own_ref[pl.ds(p * rows + r, local, stride=per), :]

    picks = []
    for p in range(box):
        wanted = ooff + p
        wanted = jnp.where(wanted >= planes, wanted - planes, wanted)
        picks.append((plane_ids == wanted).astype(jnp.float32).astype(jnp.bfloat16))
    picks = jnp.concatenate(picks, axis=0)
    for r in range(rows):
        cols = pl.ds(r * depth, depth)
        pot_hi, pot_lo = split(pot_ref[pl.ds(r, planes, stride=rows), :])
        pots = dot(picks, pot_hi) + dot(picks, pot_lo)
        for p in range(box):
            o = piece(p, r)
            up = piece(p, r - 1) if r > 0 else above_ref[pl.ds(p, local, stride=box), :]
            down = piece(p, r + 1) if r < rows - 1 else below_ref[pl.ds(p, local, stride=box), :]
            zl = jnp.where(lane == 0, 0.0, pltpu.roll(o, 1, axis=1))
            zr = jnp.where(lane == depth - 1, 0.0, pltpu.roll(o, depth - 1, axis=1))
            pot = pots[p * local : (p + 1) * local]
            u = -0.5 * (up + down + zl + zr - 6.0 * o) + pot * o - penalty * o
            base = u
            if p > 0:
                base = base - 0.5 * piece(p - 1, r)
            if p < box - 1:
                base = base - 0.5 * piece(p + 1, r)
            base_ref[pl.ds(p * local, local), cols] = base
            for value, at in ((u, p * local), (o, (box + p) * local)):
                x_hi, x_lo = split(value)
                hi_ref[pl.ds(at, local), cols] = x_hi
                lo_ref[pl.ds(at, local), cols] = x_lo
    diff = ooff - row_ref[...]
    total_ref[...] = masked_sum(box, planes, diff, hi_ref, lo_ref, hi_ref, lo_ref, box * local)


def side_kernel(
    box, rows, planes, volume,
    left_ref, right_ref, own_total_ref, hi_ref, lo_ref, ooff_ref, soff_ref,
    total_ref, s_hi_ref, s_lo_ref,
):
    per = box * rows
    side = left_ref.shape[0] // per
    depth = left_ref.shape[1]
    width = soff_ref.shape[1]
    local = ooff_ref.shape[0]
    for p in range(box):
        if width > 2 * side:
            pad = pl.ds(p * width + 2 * side, width - 2 * side)
            s_hi_ref[pad, :] = jnp.zeros((width - 2 * side, rows * depth), jnp.bfloat16)
            s_lo_ref[pad, :] = jnp.zeros((width - 2 * side, rows * depth), jnp.bfloat16)
        for r in range(rows):
            cols = pl.ds(r * depth, depth)
            for ref, at in ((left_ref, 0), (right_ref, side)):
                x_hi, x_lo = split(ref[pl.ds(p * rows + r, side, stride=per), :])
                s_hi_ref[pl.ds(p * width + at, side), cols] = x_hi
                s_lo_ref[pl.ds(p * width + at, side), cols] = x_lo
    diff = ooff_ref[...] - soff_ref[...]
    total = masked_sum(box, planes, diff, hi_ref, lo_ref, s_hi_ref, s_lo_ref, 0)
    total_ref[:, pl.ds(0, local)] = volume * own_total_ref[...]
    total_ref[:, pl.ds(local, width)] = volume * total


def mix_kernel(
    box, rows, planes,
    band_ref, base_ref, hi_ref, lo_ref, s_hi_ref, s_lo_ref, ooff_ref, row_ref, soff_ref,
    out_ref,
    own_hi, own_lo, side_hi, side_lo,
):
    per = box * rows
    local = ooff_ref.shape[0]
    width = soff_ref.shape[1]
    depth = out_ref.shape[1]
    ooff = ooff_ref[...]
    for diff, start, to_hi, to_lo in (
        (ooff - row_ref[...], 0, own_hi, own_lo),
        (ooff - soff_ref[...], local, side_hi, side_lo),
    ):
        size = diff.shape[1]
        masks = delta_masks(box, planes, diff)
        band = band_ref[:, pl.ds(start, size)]
        for k in range(1 - box, box):
            x_hi, x_lo = split(jnp.where(masks[k], band, 0.0))
            for p in range(box):
                q = p + k
                if 0 <= q < box:
                    to_hi[pl.ds(p * local, local), pl.ds(q * size, size)] = x_hi
                    to_lo[pl.ds(p * local, local), pl.ds(q * size, size)] = x_lo
    own = pl.ds(box * local, box * local)
    r_hi, r_lo = hi_ref[own, :], lo_ref[own, :]
    update = base_ref[...] - (
        dot(own_hi[...], r_hi) + dot(own_hi[...], r_lo) + dot(own_lo[...], r_hi)
        + dot(side_hi[...], s_hi_ref[...]) + dot(side_hi[...], s_lo_ref[...])
        + dot(side_lo[...], s_hi_ref[...])
    )
    for p in range(box):
        for r in range(rows):
            out_ref[pl.ds(p * rows + r, local, stride=per), :] = update[
                p * local : (p + 1) * local, r * depth : (r + 1) * depth
            ]


def sub_edges(cells):
    count = lax.axis_size("sub")
    up = [(i, i + 1) for i in range(count - 1)]
    down = [(i + 1, i) for i in range(count - 1)]
    rows = cells.shape[2]
    above = lax.ppermute(cells[:, :, rows - 1], "sub", up)
    below = lax.ppermute(cells[:, :, 0], "sub", down)
    return above, below


def sub_sum(part):
    count = lax.axis_size("sub")
    step = 1
    while step < count:
        part = part + lax.ppermute(part, "sub", [(i, i ^ step) for i in range(count)])
        step *= 2
    return part


def body(coeffs, offsets, potential):
    n = lax.axis_size("fn")
    e = lax.axis_index("fn")
    local, box, rows, depth = coeffs.shape
    planes = potential.shape[0]
    cells = rows * depth
    m = local // n
    h = -(-(KMAX - 1) // n)
    side = h * n
    volume = 1.0 / (box * 16 * 128)

    got = lax.all_to_all(coeffs.reshape(n, m, box, rows, depth), "fn", 0, 0, tiled=True)
    left = lax.ppermute(got[:, m - h :], "fn", [(i, (i + 1) % n) for i in range(n)])
    right = lax.ppermute(got[:, :h], "fn", [((i + 1) % n, i) for i in range(n)])
    above, below = sub_edges(got.reshape(local, box, rows, depth))

    offs = offsets.reshape(local, n)
    offs = jnp.concatenate([offs[local - h :], offs, offs[:h]], axis=0)
    woff = lax.dynamic_slice_in_dim(offs, m * e, m + 2 * h, axis=0)
    ooff = woff[h : h + m].T.reshape(local, 1)
    row = ooff.reshape(1, local)
    width = -(-2 * side // 128) * 128
    soff = jnp.concatenate(
        [
            woff[:h].T.reshape(1, side),
            woff[h + m :].T.reshape(1, side),
            jnp.full((1, width - 2 * side), -8 * planes, jnp.int32),
        ],
        axis=1,
    )
    params = pltpu.CompilerParams(vmem_limit_bytes=28 * 2**20)
    f32, bf16 = jnp.float32, jnp.bfloat16
    shape = jax.ShapeDtypeStruct
    full = (2 * box * local, cells)
    own_total, base, hi, lo = pl.pallas_call(
        functools.partial(own_kernel, box, rows, planes),
        out_shape=(
            shape((local, local), f32), shape((box * local, cells), f32),
            shape(full, bf16), shape(full, bf16),
        ),
        in_specs=[VMEM] * 6,
        out_specs=(VMEM,) * 4,
        compiler_params=params,
        cost_estimate=pl.CostEstimate(
            flops=12 * box * box * local * local * cells, bytes_accessed=8 * 2**20, transcendentals=0
        ),
        name="own",
    )(
        got.reshape(-1, depth), above.reshape(-1, depth), below.reshape(-1, depth),
        potential.reshape(-1, depth), ooff, row,
    )
    total, s_hi, s_lo = pl.pallas_call(
        functools.partial(side_kernel, box, rows, planes, volume),
        out_shape=(
            shape((local, local + width), f32),
            shape((box * width, cells), bf16), shape((box * width, cells), bf16),
        ),
        in_specs=[VMEM] * 7,
        out_specs=(VMEM,) * 3,
        compiler_params=params,
        name="side",
    )(left.reshape(-1, depth), right.reshape(-1, depth), own_total, hi, lo, ooff, soff)
    band = sub_sum(total)
    update = pl.pallas_call(
        functools.partial(mix_kernel, box, rows, planes),
        out_shape=shape((local * box * rows, depth), f32),
        in_specs=[VMEM] * 9,
        out_specs=VMEM,
        scratch_shapes=[pltpu.VMEM((box * local, box * local), bf16)] * 2
        + [pltpu.VMEM((box * local, box * width), bf16)] * 2,
        compiler_params=params,
        name="mix",
    )(band, base, hi, lo, s_hi, s_lo, ooff, row, soff)
    back = lax.all_to_all(update.reshape(n, m, box, rows, depth), "fn", 0, 0, tiled=True)
    return back.reshape(local, box, rows, depth)


def solution(mesh):
    return jax.shard_map(
        body,
        mesh=mesh,
        in_specs=(P("fn", None, "sub", None), P(), P(None, "sub", None)),
        out_specs=P("fn", None, "sub", None),
        check_vma=False,
    )
```

time: 109 us -> 100 us (0.917)
  Pallas kernels: 16.1 us -> 7.94 us
  starting transfers between devices: 15.7 us -> 18.7 us
  other arithmetic: 2.36 us -> 0.21 us
  blocking collectives: 30 us -> 28.2 us
    ppermute x1, waiting for transfers between devices: 0.15 us -> 9.69 us  [body(): lax.ppermute(got[:, m - h:], 'fn', [(i, (i + 1) % n) for i in range(n)])]
    ppermute x1, waiting for transfers between devices: 10.1 us -> 2.17 us  [body(): right = lax.ppermute(got[:, :h], 'fn', [((i + 1) % n, i) for i in range(n)])]
    pallas_call x1 -> x2, Pallas kernels: 11.1 us -> 5.77 us  [the longest x1 3.54 us: body(): pl.pallas_call(functools.partial(own_kernel, box, rows, planes), out_shap...]
    pallas_call x1, Pallas kernels: 5.04 us -> 2.17 us  [body(): pl.pallas_call(functools.partial(mix_kernel, box, rows, planes), out_shap...]
    ppermute x2, starting transfers between devices: 1.61 us -> 3.89 us  [sub_sum(): lax.ppermute(part, 'sub', [(i, i ^ step) for i in range(count)])]
    all_to_all x1, blocking collectives: 30 us -> 28.2 us  [body(): lax.all_to_all(update.reshape(n, m, box, rows, depth), 'fn', 0, 0, tiled=...]
    ppermute x1, starting transfers between devices: 3.05 us -> 1.29 us  [sub_edges(): above = lax.ppermute(cells[:, :, rows - 1], 'sub', up)]
    add x2, other arithmetic: 1.59 us -> 0.03 us  [sub_sum(): part + lax.ppermute(part, 'sub', [(i, i ^ step) for i in range(count)])]
  transfers between devices with their start and end apart: 7 -> 7, of which waited for: 6 -> 5; matrix products, arithmetic and copies ran while one was open for 3% -> 1% of each run, Pallas kernels for 0% -> 4%
where the time goes in v2:
time: 100 us; the launch traced here: 99.9 us
  waiting for transfers between devices  40.8 us (41%)
  blocking collectives  28.2 us (28%)
  starting transfers between devices  18.7 us (19%)
  Pallas kernels  7.94 us (8%)
  local copies, waits for them, and re-layouts  3.91 us (4%)
    all_to_all x1, blocking collectives, body(): lax.all_to_all(update.reshape(n, m, box, rows, depth), 'fn', 0, 0, tiled=...  28.2 us
    all_to_all x1, waiting for transfers between devices, body(): lax.all_to_all(coeffs.reshape(n, m, box, rows, depth), 'fn', 0, 0, tiled=...  24.2 us
    ppermute x1, waiting for transfers between devices, body(): lax.ppermute(got[:, m - h:], 'fn', [(i, (i + 1) % n) for i in range(n)])  9.69 us
    all_to_all x1, starting transfers between devices, body(): lax.all_to_all(coeffs.reshape(n, m, box, rows, depth), 'fn', 0, 0, tiled=...  7.28 us
    ppermute x2, waiting for transfers between devices, sub_sum(): lax.ppermute(part, 'sub', [(i, i ^ step) for i in range(count)])  4.8 us
    ppermute x2, starting transfers between devices, sub_sum(): lax.ppermute(part, 'sub', [(i, i ^ step) for i in range(count)])  3.89 us
    pallas_call x1, Pallas kernels, body(): pl.pallas_call(functools.partial(own_kernel, box, rows, planes), out_shap...  3.54 us
    ppermute x1, starting transfers between devices, body(): right = lax.ppermute(got[:, :h], 'fn', [((i + 1) % n, i) for i in range(n)])  3.3 us
  transfers between devices with their start and end apart: 7, of which 5 were waited for; matrix products, arithmetic and copies ran while one was open for 1% of the time, Pallas kernels for 4%

profile of v2, /device:TPU:0, one launch (start us, length us, event | category | flops | bytes accessed | tf_op | source)
XLA Modules:
  0.0 99.9 jit_solution(12298070656706162612)
XLA Ops:
  0.0 7.3 %all-to-all-start = ((f32[8,16,4,4,128]{4,3,2,1,0:T(4,128)}), f32[8,16,4,4,128]{4,3,2,1,0:T(4,128)S(1)}, u32[]{:S(2)}, u32[]{:S(2)}) async-start(f32[8,16,4,4,128]{4,3,2,1,0:T(4,128)} %bitcast.33), calls=%async_computation | async-start | bytes 2097152 | tf_op jit(solution)/shard_map/all_to_all | solution.py:201
  7.3 0.0 copy-start.1
  7.3 0.7 copy-done.1
  8.0 0.1 reshape.68
  8.1 0.1 fusion.4
  8.1 0.1 slice.54
  8.2 0.1 copy.22
  8.3 0.1 slice.56
  8.4 0.1 copy.24
  8.5 0.1 fusion.1
  8.6 0.1 slice_bitcast_fusion.2
  8.7 0.1 reshape.74.ooff_ref
  8.8 0.1 reshape_reshape.3.row_ref
  8.9 24.2 %all-to-all-done = f32[8,16,4,4,128]{4,3,2,1,0:T(4,128)S(1)} async-done(((f32[8,16,4,4,128]{4,3,2,1,0:T(4,128)}), f32[8,16,4,4,128]{4,3,2,1,0:T(4,128)S(1)}, u32[]{:S(2)}, u32[]{:S(2)}) %all-to-all-start) | async-done | bytes 1048608 | tf_op jit(solution)/shard_map/all_to_all | solution.py:201
  33.0 1.2 %fusion.2 = (f32[128,4,1,128]{3,2,1,0:T(1,128)}, f32[128,4,1,128]{3,2,1,0:T(1,128)}) fusion(f32[128,4,4,128]{3,2,1,0:T(4,128)S(1)} %bitcast.24), kind=kLoop, calls=%fused_computation.9 | loop fusion | bytes 1048576 | tf_op jit(solution)/shard_map/slice | solution.py:177
  34.2 1.3 %collective-permute-start.2 = (f32[128,4,128]{2,1,0:T(4,128)}, f32[128,4,128]{2,1,0:T(4,128)S(1)}, u32[]{:S(2)}, u32[]{:S(2)}) collective-permute-start(f32[128,4,128]{2,1,0:T(4,128)} %bitcast.5), channel_id=1, source_target_pairs={{0,1},{1,2},{2,3},{4,5},{5,6},{6,7},{8,9},{9,10},{10,11},{12,13},{... | collective-permute-start | bytes 786440 | tf_op jit(solution)/shard_map/ppermute | solution.py:176
  35.5 0.0 copy-start
  35.6 1.4 %collective-permute-start.3 = (f32[128,4,128]{2,1,0:T(4,128)}, f32[128,4,128]{2,1,0:T(4,128)S(1)}, u32[]{:S(2)}, u32[]{:S(2)}) collective-permute-start(f32[128,4,128]{2,1,0:T(4,128)} %bitcast.7), channel_id=1, source_target_pairs={{1,0},{2,1},{3,2},{5,4},{6,5},{7,6},{9,8},{10,9},{11,10},{13,12},{... | collective-permute-start | bytes 786440 | tf_op jit(solution)/shard_map/ppermute | solution.py:177
  37.0 0.1 fusion.3
  37.0 1.5 %collective-permute-start = (f32[8,6,4,4,128]{4,3,2,1,0:T(4,128)S(1)}, f32[8,6,4,4,128]{4,3,2,1,0:T(4,128)S(1)}, u32[]{:S(2)}, u32[]{:S(2)}) collective-permute-start(f32[8,6,4,4,128]{4,3,2,1,0:T(4,128)S(1)} %get-tuple-element.22), channel_id=1, source_target_pairs={{0,4},{4,8},{8,12},{12,16},{16,20},{20,24},{24,28},{28,0},{1,5},{5... | collective-permute-start | bytes 1179656 | tf_op jit(solution)/shard_map/ppermute | solution.py:202
  38.5 3.3 %collective-permute-start.1 = (f32[8,6,4,4,128]{4,3,2,1,0:T(4,128)S(1)}, f32[8,6,4,4,128]{4,3,2,1,0:T(4,128)S(1)}, u32[]{:S(2)}, u32[]{:S(2)}) collective-permute-start(f32[8,6,4,4,128]{4,3,2,1,0:T(4,128)S(1)} %get-tuple-element.21), channel_id=1, source_target_pairs={{4,0},{8,4},{12,8},{16,12},{20,16},{24,20},{28,24},{0,28},{5,1},{9... | collective-permute-start | bytes 1179656 | tf_op jit(solution)/shard_map/ppermute | solution.py:203
  41.8 0.1 slice_bitcast_fusion.1
  41.9 0.1 reshape.70
  42.0 0.1 reshape.71
  42.1 0.1 bitcast_add_fusion.soff_ref
  42.1 0.0 collective-permute-done.2
  42.1 0.0 collective-permute-done.3
  42.1 0.0 copy-done
  42.2 3.5 %own.1 = (f32[128,128]{1,0:T(8,128)S(1)}, f32[512,512]{1,0:T(8,128)S(1)}, bf16[1024,512]{1,0:T(8,128)(2,1)S(1)}, bf16[1024,512]{1,0:T(8,128)(2,1)S(1)}) custom-call(f32[2048,128]{1,0:T(8,128)S(1)} %bitcast.25, f32[512,128]{1,0:T(8,128)S(1)} %bitcast.30, f32[512,128]{1,0:T(8,128)S(1)} %bitcast.31, f32[512,128]{1,0:T(8,128)S(1)} %bitcast.29, ...), custom_call_target="tpu_custom_call" | custom-call | flops 1610612736 | bytes 8388608 | tf_op jit(solution)/shard_map/own/pallas_call | solution.py:224
  45.7 9.7 %collective-permute-done = f32[8,6,4,4,128]{4,3,2,1,0:T(4,128)S(1)} collective-permute-done((f32[8,6,4,4,128]{4,3,2,1,0:T(4,128)S(1)}, f32[8,6,4,4,128]{4,3,2,1,0:T(4,128)S(1)}, u32[]{:S(2)}, u32[]{:S(2)}) %collective-permute-start) | collective-permute-done | bytes 393248 | tf_op jit(solution)/shard_map/ppermute | solution.py:202
  55.4 2.2 %collective-permute-done.1 = f32[8,6,4,4,128]{4,3,2,1,0:T(4,128)S(1)} collective-permute-done((f32[8,6,4,4,128]{4,3,2,1,0:T(4,128)S(1)}, f32[8,6,4,4,128]{4,3,2,1,0:T(4,128)S(1)}, u32[]{:S(2)}, u32[]{:S(2)}) %collective-permute-start.1) | collective-permute-done | bytes 393248 | tf_op jit(solution)/shard_map/ppermute | solution.py:203
  57.6 2.2 %side.1 = (f32[128,256]{1,0:T(8,128)S(1)}, bf16[512,512]{1,0:T(8,128)(2,1)S(1)}, bf16[512,512]{1,0:T(8,128)(2,1)S(1)}) custom-call(f32[768,128]{1,0:T(8,128)S(1)} %bitcast.27, f32[768,128]{1,0:T(8,128)S(1)} %bitcast.28, f32[128,128]{1,0:T(8,128)S(1)} %get-tuple-element.12.own_total_ref, bf16[1024,512]{1,0:T(8,128)(2,1)S(1)} %get-tuple-element.13.hi_ref, ...), custom_call_target="tpu_custom_call" | custom-call | tf_op jit(solution)/shard_map/side/pallas_call | solution.py:241
  59.8 1.3 %collective-permute-start.4 = (f32[128,256]{1,0:T(8,128)S(1)}, f32[128,256]{1,0:T(8,128)S(1)}, u32[]{:S(2)}, u32[]{:S(2)}) collective-permute-start(f32[128,256]{1,0:T(8,128)S(1)} %get-tuple-element.15), channel_id=1, source_target_pairs={{0,1},{1,0},{2,3},{3,2},{4,5},{5,4},{6,7},{7,6},{8,9},{9,8},{10,11... | collective-permute-start | bytes 393224 | tf_op jit(solution)/shard_map/ppermute | solution.py:185
  61.0 1.0 collective-permute-done.4
  62.1 2.6 %collective-permute-start.5 = (f32[128,256]{1,0:T(8,128)S(1)}, f32[128,256]{1,0:T(8,128)S(1)}, u32[]{:S(2)}, u32[]{:S(2)}) collective-permute-start(f32[128,256]{1,0:T(8,128)S(1)} %add.10), channel_id=1, source_target_pairs={{0,2},{1,3},{2,0},{3,1},{4,6},{5,7},{6,4},{7,5},{8,10},{9,11},{10,... | collective-permute-start | bytes 393224 | tf_op jit(solution)/shard_map/ppermute | solution.py:185
  64.7 3.8 %collective-permute-done.5 = f32[128,256]{1,0:T(8,128)S(1)} collective-permute-done((f32[128,256]{1,0:T(8,128)S(1)}, f32[128,256]{1,0:T(8,128)S(1)}, u32[]{:S(2)}, u32[]{:S(2)}) %collective-permute-start.5) | collective-permute-done | bytes 131104 | tf_op jit(solution)/shard_map/ppermute | solution.py:185
  68.5 2.2 %mix.1 = f32[2048,128]{1,0:T(8,128)S(1)} custom-call(f32[128,256]{1,0:T(8,128)S(1)} %add.11.band_ref, f32[512,512]{1,0:T(8,128)S(1)} %get-tuple-element.16.base_ref, bf16[1024,512]{1,0:T(8,128)(2,1)S(1)} %get-tuple-element.13.hi_ref, bf16[1024,512]{1,0:T(8,128)(2,1)S(1)} %get-tuple-element.14.lo_ref, bf16[512,512]{1,0:T(8,128)(2,1)S(1)} %get-tuple-element.17.s_hi_ref, ...), custom_call_target="tpu_custom_call" | custom-call | tf_op jit(solution)/shard_map/mix/pallas_call | solution.py:253
  70.7 28.2 %all_to_all.10 = f32[8,16,4,4,128]{4,3,2,1,0:T(4,128)S(1)} all-to-all(f32[8,16,4,4,128]{4,3,2,1,0:T(4,128)S(1)} %bitcast.26), channel_id=1, replica_groups=mesh['fn'=8,'sub'=4] {'fn'}, dimensions={0} | all-to-all | bytes 2097152 | tf_op jit(solution)/shard_map/all_to_all | solution.py:263
  98.9 1.0 copy.31
  (4 shorter events, 0.1 us)
Async XLA Ops:
  0.0 33.0 %all-to-all-start = ((f32[8,16,4,4,128]{4,3,2,1,0:T(4,128)}), f32[8,16,4,4,128]{4,3,2,1,0:T(4,128)S(1)}, u32[]{:S(2)}, u32[]{:S(2)}) async-start(f32[8,16,4,4,128]{4,3,2,1,0:T(4,128)} %bitcast.33), calls=%async_computation | async-start | bytes 2097152 | tf_op jit(solution)/shard_map/all_to_all | solution.py:201
  7.3 0.7 copy-start.1
  34.2 7.9 %collective-permute-start.2 = (f32[128,4,128]{2,1,0:T(4,128)}, f32[128,4,128]{2,1,0:T(4,128)S(1)}, u32[]{:S(2)}, u32[]{:S(2)}) collective-permute-start(f32[128,4,128]{2,1,0:T(4,128)} %bitcast.5), channel_id=1, source_target_pairs={{0,1},{1,2},{2,3},{4,5},{5,6},{6,7},{8,9},{9,10},{10,11},{12,13},{... | collective-permute-start | bytes 786440 | tf_op jit(solution)/shard_map/ppermute | solution.py:176
  35.5 6.6 %copy-start = (f32[128,4,128]{2,1,0:T(4,128)S(1)}, f32[128,4,128]{2,1,0:T(4,128)}, u32[]{:S(2)}) copy-start(f32[128,4,128]{2,1,0:T(4,128)} %param.5) | copy-start | bytes 786436
  35.6 6.6 %collective-permute-start.3 = (f32[128,4,128]{2,1,0:T(4,128)}, f32[128,4,128]{2,1,0:T(4,128)S(1)}, u32[]{:S(2)}, u32[]{:S(2)}) collective-permute-start(f32[128,4,128]{2,1,0:T(4,128)} %bitcast.7), channel_id=1, source_target_pairs={{1,0},{2,1},{3,2},{5,4},{6,5},{7,6},{9,8},{10,9},{11,10},{13,12},{... | collective-permute-start | bytes 786440 | tf_op jit(solution)/shard_map/ppermute | solution.py:177
  37.0 18.3 %collective-permute-start = (f32[8,6,4,4,128]{4,3,2,1,0:T(4,128)S(1)}, f32[8,6,4,4,128]{4,3,2,1,0:T(4,128)S(1)}, u32[]{:S(2)}, u32[]{:S(2)}) collective-permute-start(f32[8,6,4,4,128]{4,3,2,1,0:T(4,128)S(1)} %get-tuple-element.22), channel_id=1, source_target_pairs={{0,4},{4,8},{8,12},{12,16},{16,20},{20,24},{24,28},{28,0},{1,5},{5... | collective-permute-start | bytes 1179656 | tf_op jit(solution)/shard_map/ppermute | solution.py:202
  38.5 19.0 %collective-permute-start.1 = (f32[8,6,4,4,128]{4,3,2,1,0:T(4,128)S(1)}, f32[8,6,4,4,128]{4,3,2,1,0:T(4,128)S(1)}, u32[]{:S(2)}, u32[]{:S(2)}) collective-permute-start(f32[8,6,4,4,128]{4,3,2,1,0:T(4,128)S(1)} %get-tuple-element.21), channel_id=1, source_target_pairs={{4,0},{8,4},{12,8},{16,12},{20,16},{24,20},{28,24},{0,28},{5,1},{9... | collective-permute-start | bytes 1179656 | tf_op jit(solution)/shard_map/ppermute | solution.py:203
  59.8 2.2 %collective-permute-start.4 = (f32[128,256]{1,0:T(8,128)S(1)}, f32[128,256]{1,0:T(8,128)S(1)}, u32[]{:S(2)}, u32[]{:S(2)}) collective-permute-start(f32[128,256]{1,0:T(8,128)S(1)} %get-tuple-element.15), channel_id=1, source_target_pairs={{0,1},{1,0},{2,3},{3,2},{4,5},{5,4},{6,7},{7,6},{8,9},{9,8},{10,11... | collective-permute-start | bytes 393224 | tf_op jit(solution)/shard_map/ppermute | solution.py:185
  62.1 6.4 %collective-permute-start.5 = (f32[128,256]{1,0:T(8,128)S(1)}, f32[128,256]{1,0:T(8,128)S(1)}, u32[]{:S(2)}, u32[]{:S(2)}) collective-permute-start(f32[128,256]{1,0:T(8,128)S(1)} %add.10), channel_id=1, source_target_pairs={{0,2},{1,3},{2,0},{3,1},{4,6},{5,7},{6,4},{7,5},{8,10},{9,11},{10,... | collective-permute-start | bytes 393224 | tf_op jit(solution)/shard_map/ppermute | solution.py:185

commit v3 on v2

--- a/solution.py
+++ b/solution.py
@@ -6,6 +6,7 @@
 from jax.experimental import pallas as pl
 from jax.experimental.pallas import tpu as pltpu
 from jax.sharding import PartitionSpec as P
+
 
 KMAX = 46
 penalty = 0.5
@@ -137,7 +138,6 @@
 ):
     per = box * rows
     local = ooff_ref.shape[0]
-    width = soff_ref.shape[1]
     depth = out_ref.shape[1]
     ooff = ooff_ref[...]
     for diff, start, to_hi, to_lo in (
@@ -199,9 +199,10 @@
     volume = 1.0 / (box * 16 * 128)
 
     got = lax.all_to_all(coeffs.reshape(n, m, box, rows, depth), "fn", 0, 0, tiled=True)
-    left = lax.ppermute(got[:, m - h :], "fn", [(i, (i + 1) % n) for i in range(n)])
-    right = lax.ppermute(got[:, :h], "fn", [((i + 1) % n, i) for i in range(n)])
-    above, below = sub_edges(got.reshape(local, box, rows, depth))
+    tail, head, after = lax.optimization_barrier((got[:, m - h :], got[:, :h], got))
+    left = lax.ppermute(tail, "fn", [(i, (i + 1) % n) for i in range(n)])
+    right = lax.ppermute(head, "fn", [((i + 1) % n, i) for i in range(n)])
+    above, below = sub_edges(after.reshape(local, box, rows, depth))
 
     offs = offsets.reshape(local, n)
     offs = jnp.concatenate([offs[local - h :], offs, offs[:h]], axis=0)

time: 100 us -> 95.1 us (0.951)
  waiting for transfers between devices: 40.8 us -> 37.9 us
  starting transfers between devices: 18.7 us -> 16.6 us
    ppermute x2, waiting for transfers between devices: 11.9 us -> 3.48 us  [the longest x1 2.2 us: body(): right = lax.ppermute(head, 'fn', [((i + 1) % n, i) for i in range(n)])]
    ppermute x1, waiting for transfers between devices: 0.01 us -> 3.76 us  [sub_edges(): below = lax.ppermute(cells[:, :, 0], 'sub', down)]
    ppermute x2, starting transfers between devices: 3.89 us -> 2.01 us  [sub_sum(): lax.ppermute(part, 'sub', [(i, i ^ step) for i in range(count)])]
    ppermute x2, waiting for transfers between devices: 4.8 us -> 6.45 us  [sub_sum(): lax.ppermute(part, 'sub', [(i, i ^ step) for i in range(count)])]
  transfers between devices with their start and end apart: 7 -> 7, of which waited for: 5 -> 6; matrix products, arithmetic and copies ran while one was open for 1% -> 2% of each run, Pallas kernels for 4% -> 4%
where the time goes in v3:
time: 95.1 us; the launch traced here: 94.9 us
  waiting for transfers between devices  37.9 us (40%)
  blocking collectives  28.1 us (30%)
  starting transfers between devices  16.6 us (17%)
  Pallas kernels  8.02 us (8%)
  local copies, waits for them, and re-layouts  3.9 us (4%)
    all_to_all x1, blocking collectives, body(): lax.all_to_all(update.reshape(n, m, box, rows, depth), 'fn', 0, 0, tiled=...  28.1 us
    all_to_all x1, waiting for transfers between devices, body(): lax.all_to_all(coeffs.reshape(n, m, box, rows, depth), 'fn', 0, 0, tiled=...  24.2 us
    all_to_all x1, starting transfers between devices, body(): lax.all_to_all(coeffs.reshape(n, m, box, rows, depth), 'fn', 0, 0, tiled=...  7.28 us
    ppermute x2, waiting for transfers between devices, sub_sum(): lax.ppermute(part, 'sub', [(i, i ^ step) for i in range(count)])  6.45 us
    ppermute x1, waiting for transfers between devices, sub_edges(): below = lax.ppermute(cells[:, :, 0], 'sub', down)  3.76 us
    pallas_call x1, Pallas kernels, body(): pl.pallas_call(functools.partial(own_kernel, box, rows, planes), out_shap...  3.61 us
    ppermute x1, starting transfers between devices, body(): right = lax.ppermute(head, 'fn', [((i + 1) % n, i) for i in range(n)])  3.3 us
    pallas_call x1, Pallas kernels, body(): pl.pallas_call(functools.partial(side_kernel, box, rows, planes, volume),...  2.22 us
  transfers between devices with their start and end apart: 7, of which 6 were waited for; matrix products, arithmetic and copies ran while one was open for 2% of the time, Pallas kernels for 4%

profile of v3, /device:TPU:0, one launch (start us, length us, event | category | flops | bytes accessed | tf_op | source)
XLA Modules:
  0.0 94.9 jit_solution(3421938091529204081)
XLA Ops:
  0.0 7.3 %all-to-all-start = ((f32[8,16,4,4,128]{4,3,2,1,0:T(4,128)}), f32[8,16,4,4,128]{4,3,2,1,0:T(4,128)S(1)}, u32[]{:S(2)}, u32[]{:S(2)}) async-start(f32[8,16,4,4,128]{4,3,2,1,0:T(4,128)} %bitcast.33), calls=%async_computation | async-start | bytes 2097152 | tf_op jit(solution)/shard_map/all_to_all | solution.py:201
  7.3 0.0 copy-start.1
  7.3 0.7 copy-done.1
  8.0 0.1 reshape.68
  8.1 0.1 fusion.4
  8.1 0.1 slice.56
  8.2 0.1 copy.24
  8.3 0.1 slice.54
  8.4 0.1 copy.22
  8.5 0.1 fusion.1
  8.6 0.1 slice_bitcast_fusion.2
  8.7 0.1 reshape_reshape.3.row_ref
  8.8 0.1 reshape.74.ooff_ref
  8.9 24.2 %all-to-all-done = f32[8,16,4,4,128]{4,3,2,1,0:T(4,128)S(1)} async-done(((f32[8,16,4,4,128]{4,3,2,1,0:T(4,128)}), f32[8,16,4,4,128]{4,3,2,1,0:T(4,128)S(1)}, u32[]{:S(2)}, u32[]{:S(2)}) %all-to-all-start) | async-done | bytes 1048608 | tf_op jit(solution)/shard_map/all_to_all | solution.py:201
  33.0 0.1 fusion.3
  33.1 1.5 %collective-permute-start = (f32[8,6,4,4,128]{4,3,2,1,0:T(4,128)S(1)}, f32[8,6,4,4,128]{4,3,2,1,0:T(4,128)S(1)}, u32[]{:S(2)}, u32[]{:S(2)}) collective-permute-start(f32[8,6,4,4,128]{4,3,2,1,0:T(4,128)S(1)} %get-tuple-element.15), channel_id=1, source_target_pairs={{0,4},{4,8},{8,12},{12,16},{16,20},{20,24},{24,28},{28,0},{1,5},{5... | collective-permute-start | bytes 1179656 | tf_op jit(solution)/shard_map/ppermute | solution.py:203
  34.6 3.3 %collective-permute-start.1 = (f32[8,6,4,4,128]{4,3,2,1,0:T(4,128)S(1)}, f32[8,6,4,4,128]{4,3,2,1,0:T(4,128)S(1)}, u32[]{:S(2)}, u32[]{:S(2)}) collective-permute-start(f32[8,6,4,4,128]{4,3,2,1,0:T(4,128)S(1)} %get-tuple-element.16), channel_id=1, source_target_pairs={{4,0},{8,4},{12,8},{16,12},{20,16},{24,20},{28,24},{0,28},{5,1},{9... | collective-permute-start | bytes 1179656 | tf_op jit(solution)/shard_map/ppermute | solution.py:204
  37.9 0.0 copy-start
  37.9 1.2 %fusion.2 = (f32[128,4,1,128]{3,2,1,0:T(1,128)}, f32[128,4,1,128]{3,2,1,0:T(1,128)}) fusion(f32[128,4,4,128]{3,2,1,0:T(4,128)S(1)} %bitcast.24), kind=kLoop, calls=%fused_computation.9 | loop fusion | bytes 1048576 | tf_op jit(solution)/shard_map/slice | solution.py:177
  39.1 1.3 %collective-permute-start.2 = (f32[128,4,128]{2,1,0:T(4,128)}, f32[128,4,128]{2,1,0:T(4,128)S(1)}, u32[]{:S(2)}, u32[]{:S(2)}) collective-permute-start(f32[128,4,128]{2,1,0:T(4,128)} %bitcast.5), channel_id=1, source_target_pairs={{0,1},{1,2},{2,3},{4,5},{5,6},{6,7},{8,9},{9,10},{10,11},{12,13},{... | collective-permute-start | bytes 786440 | tf_op jit(solution)/shard_map/ppermute | solution.py:176
  40.4 1.3 %collective-permute-start.3 = (f32[128,4,128]{2,1,0:T(4,128)}, f32[128,4,128]{2,1,0:T(4,128)S(1)}, u32[]{:S(2)}, u32[]{:S(2)}) collective-permute-start(f32[128,4,128]{2,1,0:T(4,128)} %bitcast.7), channel_id=1, source_target_pairs={{1,0},{2,1},{3,2},{5,4},{6,5},{7,6},{9,8},{10,9},{11,10},{13,12},{... | collective-permute-start | bytes 786440 | tf_op jit(solution)/shard_map/ppermute | solution.py:177
  41.7 0.1 slice_bitcast_fusion.1
  41.7 0.1 reshape.70
  41.8 0.1 reshape.71
  41.9 0.1 bitcast_add_fusion.soff_ref
  42.0 0.0 collective-permute-done.2
  42.0 3.8 %collective-permute-done.3 = f32[128,4,128]{2,1,0:T(4,128)S(1)} collective-permute-done((f32[128,4,128]{2,1,0:T(4,128)}, f32[128,4,128]{2,1,0:T(4,128)S(1)}, u32[]{:S(2)}, u32[]{:S(2)}) %collective-permute-start.3) | collective-permute-done | bytes 262176 | tf_op jit(solution)/shard_map/ppermute | solution.py:177
  45.8 0.0 copy-done
  45.8 3.6 %own.1 = (f32[128,128]{1,0:T(8,128)S(1)}, f32[512,512]{1,0:T(8,128)S(1)}, bf16[1024,512]{1,0:T(8,128)(2,1)S(1)}, bf16[1024,512]{1,0:T(8,128)(2,1)S(1)}) custom-call(f32[2048,128]{1,0:T(8,128)S(1)} %bitcast.25, f32[512,128]{1,0:T(8,128)S(1)} %bitcast.30, f32[512,128]{1,0:T(8,128)S(1)} %bitcast.31, f32[512,128]{1,0:T(8,128)S(1)} %bitcast.29, ...), custom_call_target="tpu_custom_call" | custom-call | flops 1610612736 | bytes 8388608 | tf_op jit(solution)/shard_map/own/pallas_call | solution.py:225
  49.4 1.3 %collective-permute-done = f32[8,6,4,4,128]{4,3,2,1,0:T(4,128)S(1)} collective-permute-done((f32[8,6,4,4,128]{4,3,2,1,0:T(4,128)S(1)}, f32[8,6,4,4,128]{4,3,2,1,0:T(4,128)S(1)}, u32[]{:S(2)}, u32[]{:S(2)}) %collective-permute-start) | collective-permute-done | bytes 393248 | tf_op jit(solution)/shard_map/ppermute | solution.py:203
  50.7 2.2 %collective-permute-done.1 = f32[8,6,4,4,128]{4,3,2,1,0:T(4,128)S(1)} collective-permute-done((f32[8,6,4,4,128]{4,3,2,1,0:T(4,128)S(1)}, f32[8,6,4,4,128]{4,3,2,1,0:T(4,128)S(1)}, u32[]{:S(2)}, u32[]{:S(2)}) %collective-permute-start.1) | collective-permute-done | bytes 393248 | tf_op jit(solution)/shard_map/ppermute | solution.py:204
  52.9 2.2 %side.1 = (f32[128,256]{1,0:T(8,128)S(1)}, bf16[512,512]{1,0:T(8,128)(2,1)S(1)}, bf16[512,512]{1,0:T(8,128)(2,1)S(1)}) custom-call(f32[768,128]{1,0:T(8,128)S(1)} %bitcast.27, f32[768,128]{1,0:T(8,128)S(1)} %bitcast.28, f32[128,128]{1,0:T(8,128)S(1)} %get-tuple-element.18.own_total_ref, bf16[1024,512]{1,0:T(8,128)(2,1)S(1)} %get-tuple-element.19.hi_ref, ...), custom_call_target="tpu_custom_call" | custom-call | tf_op jit(solution)/shard_map/side/pallas_call | solution.py:242
  55.1 1.6 %collective-permute-start.4 = (f32[128,256]{1,0:T(8,128)S(1)}, f32[128,256]{1,0:T(8,128)S(1)}, u32[]{:S(2)}, u32[]{:S(2)}) collective-permute-start(f32[128,256]{1,0:T(8,128)S(1)} %get-tuple-element.21), channel_id=1, source_target_pairs={{0,1},{1,0},{2,3},{3,2},{4,5},{5,4},{6,7},{7,6},{8,9},{9,8},{10,11... | collective-permute-start | bytes 393224 | tf_op jit(solution)/shard_map/ppermute | solution.py:185
  56.7 1.0 %collective-permute-done.4 = f32[128,256]{1,0:T(8,128)S(1)} collective-permute-done((f32[128,256]{1,0:T(8,128)S(1)}, f32[128,256]{1,0:T(8,128)S(1)}, u32[]{:S(2)}, u32[]{:S(2)}) %collective-permute-start.4) | collective-permute-done | bytes 131104 | tf_op jit(solution)/shard_map/ppermute | solution.py:185
  57.7 0.4 collective-permute-start.5
  58.1 5.5 %collective-permute-done.5 = f32[128,256]{1,0:T(8,128)S(1)} collective-permute-done((f32[128,256]{1,0:T(8,128)S(1)}, f32[128,256]{1,0:T(8,128)S(1)}, u32[]{:S(2)}, u32[]{:S(2)}) %collective-permute-start.5) | collective-permute-done | bytes 131104 | tf_op jit(solution)/shard_map/ppermute | solution.py:185
  63.6 2.2 %mix.1 = f32[2048,128]{1,0:T(8,128)S(1)} custom-call(f32[128,256]{1,0:T(8,128)S(1)} %add.11.band_ref, f32[512,512]{1,0:T(8,128)S(1)} %get-tuple-element.22.base_ref, bf16[1024,512]{1,0:T(8,128)(2,1)S(1)} %get-tuple-element.19.hi_ref, bf16[1024,512]{1,0:T(8,128)(2,1)S(1)} %get-tuple-element.20.lo_ref, bf16[512,512]{1,0:T(8,128)(2,1)S(1)} %get-tuple-element.23.s_hi_ref, ...), custom_call_target="tpu_custom_call" | custom-call | tf_op jit(solution)/shard_map/mix/pallas_call | solution.py:254
  65.8 28.1 %all_to_all.10 = f32[8,16,4,4,128]{4,3,2,1,0:T(4,128)S(1)} all-to-all(f32[8,16,4,4,128]{4,3,2,1,0:T(4,128)S(1)} %bitcast.26), channel_id=1, replica_groups=mesh['fn'=8,'sub'=4] {'fn'}, dimensions={0} | all-to-all | bytes 2097152 | tf_op jit(solution)/shard_map/all_to_all | solution.py:264
  93.9 1.0 %copy.31 = f32[128,4,4,128]{3,2,1,0:T(4,128)} copy(f32[128,4,4,128]{3,2,1,0:T(4,128)S(1)} %bitcast.32) | data formatting | bytes 2097152
  (4 shorter events, 0.1 us)
Async XLA Ops:
  0.0 33.0 %all-to-all-start = ((f32[8,16,4,4,128]{4,3,2,1,0:T(4,128)}), f32[8,16,4,4,128]{4,3,2,1,0:T(4,128)S(1)}, u32[]{:S(2)}, u32[]{:S(2)}) async-start(f32[8,16,4,4,128]{4,3,2,1,0:T(4,128)} %bitcast.33), calls=%async_computation | async-start | bytes 2097152 | tf_op jit(solution)/shard_map/all_to_all | solution.py:201
  7.3 0.7 copy-start.1
  33.1 17.5 %collective-permute-start = (f32[8,6,4,4,128]{4,3,2,1,0:T(4,128)S(1)}, f32[8,6,4,4,128]{4,3,2,1,0:T(4,128)S(1)}, u32[]{:S(2)}, u32[]{:S(2)}) collective-permute-start(f32[8,6,4,4,128]{4,3,2,1,0:T(4,128)S(1)} %get-tuple-element.15), channel_id=1, source_target_pairs={{0,4},{4,8},{8,12},{12,16},{16,20},{20,24},{24,28},{28,0},{1,5},{5... | collective-permute-start | bytes 1179656 | tf_op jit(solution)/shard_map/ppermute | solution.py:203
  34.6 18.3 %collective-permute-start.1 = (f32[8,6,4,4,128]{4,3,2,1,0:T(4,128)S(1)}, f32[8,6,4,4,128]{4,3,2,1,0:T(4,128)S(1)}, u32[]{:S(2)}, u32[]{:S(2)}) collective-permute-start(f32[8,6,4,4,128]{4,3,2,1,0:T(4,128)S(1)} %get-tuple-element.16), channel_id=1, source_target_pairs={{4,0},{8,4},{12,8},{16,12},{20,16},{24,20},{28,24},{0,28},{5,1},{9... | collective-permute-start | bytes 1179656 | tf_op jit(solution)/shard_map/ppermute | solution.py:204
  37.9 7.9 %copy-start = (f32[128,4,128]{2,1,0:T(4,128)S(1)}, f32[128,4,128]{2,1,0:T(4,128)}, u32[]{:S(2)}) copy-start(f32[128,4,128]{2,1,0:T(4,128)} %param.5) | copy-start | bytes 786436
  39.1 2.9 %collective-permute-start.2 = (f32[128,4,128]{2,1,0:T(4,128)}, f32[128,4,128]{2,1,0:T(4,128)S(1)}, u32[]{:S(2)}, u32[]{:S(2)}) collective-permute-start(f32[128,4,128]{2,1,0:T(4,128)} %bitcast.5), channel_id=1, source_target_pairs={{0,1},{1,2},{2,3},{4,5},{5,6},{6,7},{8,9},{9,10},{10,11},{12,13},{... | collective-permute-start | bytes 786440 | tf_op jit(solution)/shard_map/ppermute | solution.py:176
  40.4 5.4 %collective-permute-start.3 = (f32[128,4,128]{2,1,0:T(4,128)}, f32[128,4,128]{2,1,0:T(4,128)S(1)}, u32[]{:S(2)}, u32[]{:S(2)}) collective-permute-start(f32[128,4,128]{2,1,0:T(4,128)} %bitcast.7), channel_id=1, source_target_pairs={{1,0},{2,1},{3,2},{5,4},{6,5},{7,6},{9,8},{10,9},{11,10},{13,12},{... | collective-permute-start | bytes 786440 | tf_op jit(solution)/shard_map/ppermute | solution.py:177
  55.1 2.6 %collective-permute-start.4 = (f32[128,256]{1,0:T(8,128)S(1)}, f32[128,256]{1,0:T(8,128)S(1)}, u32[]{:S(2)}, u32[]{:S(2)}) collective-permute-start(f32[128,256]{1,0:T(8,128)S(1)} %get-tuple-element.21), channel_id=1, source_target_pairs={{0,1},{1,0},{2,3},{3,2},{4,5},{5,4},{6,7},{7,6},{8,9},{9,8},{10,11... | collective-permute-start | bytes 393224 | tf_op jit(solution)/shard_map/ppermute | solution.py:185
  57.7 5.8 %collective-permute-start.5 = (f32[128,256]{1,0:T(8,128)S(1)}, f32[128,256]{1,0:T(8,128)S(1)}, u32[]{:S(2)}, u32[]{:S(2)}) collective-permute-start(f32[128,256]{1,0:T(8,128)S(1)} %add.10), channel_id=1, source_target_pairs={{0,2},{1,3},{2,0},{3,1},{4,6},{5,7},{6,4},{7,5},{8,10},{9,11},{10,... | collective-permute-start | bytes 393224 | tf_op jit(solution)/shard_map/ppermute | solution.py:185
